TPU v7x, 32 devices: a whole 2x2x4 slice. The times are simulated.
32 devices in a mesh: rows: 4 (over y, core), chan: 8 (over z, x).
Axes of the slice: x: 2, y: 2, z: 4, core: 2. Of those that a mesh axis runs over, the one named last changes fastest.
Arguments:
- features: bfloat16 [1024, 16, 128], P('chan', 'rows'), may hold values from -6 to 6
- hidden: bfloat16 [1024, 16, 128], P('chan', 'rows'), may hold values from -1 to 1
- w_update: bfloat16 [3, 3, 1024, 2048], P(None, None, 'chan'), may hold values from -0.046875 to 0.046875
- w_reset: bfloat16 [3, 3, 1024, 2048], P(None, None, 'chan'), may hold values from -0.046875 to 0.046875
- w_cand: bfloat16 [3, 3, 1024, 2048], P(None, None, 'chan'), may hold values from -0.046875 to 0.046875
- b_update: float32 [1024], P('chan'), may hold values from -1 to 1
- b_reset: float32 [1024], P('chan'), may hold values from -1 to 1
- b_cand: float32 [1024], P('chan'), may hold values from -1 to 1
Outputs:
- new_hidden: bfloat16 [1024, 16, 128], P('chan', 'rows')
All inputs are finite; a program needn't handle non-finite values.
Results may differ from a plain program's by a relative error of at most 0.0018.
Values may be sent and summed in bfloat16 or wider, within the bound.
A program may use at most 128 MiB of HBM per device.

v0:
```python
import jax
import jax.numpy as jnp
from jax import lax
from jax.sharding import PartitionSpec as P

C_IN = 1024


def extended(block, sides, width):
    for axis, dim in sides:
        count = lax.axis_size(axis)
        forward = [(i, i + 1) for i in range(count - 1)]
        backward = [(target, source) for source, target in forward]
        low = lax.ppermute(
            lax.slice_in_dim(block, block.shape[dim] - width, None, axis=dim), axis, forward
        )
        high = lax.ppermute(lax.slice_in_dim(block, 0, width, axis=dim), axis, backward)
        block = jnp.concatenate([low, block, high], axis=dim)
    return block


def conv_rows(source, kernel):
    src_rows = source.shape[1]
    out_rows = src_rows - 2
    out_cols = source.shape[2]
    outputs = kernel.shape[2]
    inner = kernel.shape[3]
    flat = kernel.reshape(9 * outputs, inner)
    product = jnp.einsum("pk,krw->prw", flat, source, preferred_element_type=jnp.float32)
    product = product.reshape(3, 3, outputs, src_rows, out_cols)
    padded = jnp.pad(product, ((0, 0), (0, 0), (0, 0), (0, 0), (1, 1)))
    result = None
    for row_off in range(3):
        for col_off in range(3):
            term = padded[
                row_off, col_off, :, row_off : row_off + out_rows, col_off : col_off + out_cols
            ]
            result = term if result is None else result + term
    return result


def per_device(features, hidden, w_update, w_reset, w_cand, b_update, b_reset, b_cand):
    width = 1
    in_dev = features.shape[0]
    hid_dev = hidden.shape[0]
    w_gates = jnp.concatenate([w_update, w_reset], 2)
    local = jnp.concatenate([features, hidden], 0)
    padded = extended(local, (("rows", 1),), width)
    x_piece = lax.all_gather(padded[:in_dev], "chan", axis=0, tiled=True)
    h_piece = lax.all_gather(padded[in_dev:], "chan", axis=0, tiled=True)
    count = x_piece.shape[0]
    gate_acc = conv_rows(x_piece, lax.slice_in_dim(w_gates, 0, count, axis=3))
    gate_acc = gate_acc + conv_rows(h_piece, lax.dynamic_slice_in_dim(w_gates, C_IN, count, 3))
    cand_acc = conv_rows(x_piece, lax.slice_in_dim(w_cand, 0, count, axis=3))
    cand_pre = cand_acc
    update = jax.nn.sigmoid(gate_acc[:hid_dev] + b_update[:, None, None])
    reset = jax.nn.sigmoid(gate_acc[hid_dev:] + b_reset[:, None, None])
    reset_hidden = (reset * hidden.astype(jnp.float32)).astype(jnp.bfloat16)
    reset_rows = extended(reset_hidden, (("rows", 1),), 1)
    piece = lax.all_gather(reset_rows, "chan", axis=0, tiled=True)
    cand_pre = cand_pre + conv_rows(
        piece, lax.dynamic_slice_in_dim(w_cand, C_IN, piece.shape[0], 3)
    )
    candidate = jnp.tanh(cand_pre + b_cand[:, None, None])
    new_hidden = (1.0 - update) * hidden.astype(jnp.float32) + update * candidate
    return new_hidden.astype(jnp.bfloat16)


def solution(mesh):
    in_specs = (
        P("chan", "rows", None),
        P("chan", "rows", None),
        P(None, None, "chan", None),
        P(None, None, "chan", None),
        P(None, None, "chan", None),
        P("chan"),
        P("chan"),
        P("chan"),
    )
    out_specs = P("chan", "rows", None)
    return jax.shard_map(
        per_device, mesh=mesh, in_specs=in_specs, out_specs=out_specs, check_vma=False
    )
```

profile of v0, /device:TPU:1, one launch (start us, length us, event | category | flops | bytes accessed | tf_op | source)
XLA Modules:
  0.0 193.8 jit_solution(2412670403156365406)
XLA Ops:
  6.5 0.0 all-gather.4.cloned.1.call-start
  6.5 1.0 copy.14
  7.6 0.0 copy-start.1
  7.6 1.1 copy.13
  8.7 4.5 %collective-permute-start = (bf16[256,1,128]{0,2,1:T(8,128)(2,1)S(1)}, bf16[256,1,128]{0,2,1:T(8,128)(2,1)S(1)}, u32[]{:S(2)}, u32[]{:S(2)}) collective-permute-start(bf16[256,1,128]{0,2,1:T(8,128)(2,1)S(1)} %get-tuple-element.9), channel_id=1, source_target_pairs={{0,8},{8,16},{16,24},{1,9},{9,17},{17,25},{2,10},{10,18},{18,26},{... | collective-permute-start | bytes 196616 | tf_op jit(solution)/shard_map/ppermute | solution.py:14
  13.2 1.9 collective-permute-start.1
  15.2 0.0 collective-permute-done
  15.2 3.6 %collective-permute-done.1 = bf16[256,1,128]{0,2,1:T(8,128)(2,1)S(1)} collective-permute-done((bf16[256,1,128]{0,2,1:T(8,128)(2,1)S(1)}, bf16[256,1,128]{0,2,1:T(8,128)(2,1)S(1)}, u32[]{:S(2)}, u32[]{:S(2)}) %collective-permute-start.1) | collective-permute-done | bytes 65568 | tf_op jit(solution)/shard_map/ppermute | solution.py:17
  18.9 0.8 fusion.54
  19.7 0.0 all-gather.4.cloned.1.call-update
  19.7 0.0 all-gather.6.cloned.1.call-start
  19.8 0.7 all-gather.6.cloned.1.call-update
  20.5 0.0 all-gather.8.cloned.1.call-start
  20.5 5.2 %constant_dynamic-update-slice_fusion.1 = bf16[3,3,256,2048]{3,2,1,0:T(8,128)(2,1)} fusion(bf16[3,3,128,2048]{3,2,1,0:T(8,128)(2,1)} %param.10), kind=kLoop, calls=%fused_computation.91 | loop fusion | bytes 9437184
  25.8 5.2 %constant_dynamic-update-slice_fusion = bf16[3,3,256,2048]{3,2,1,0:T(8,128)(2,1)} fusion(bf16[3,3,256,2048]{3,2,1,0:T(8,128)(2,1)} %constant_dynamic-update-slice_fusion.1, bf16[3,3,128,2048]{3,2,1,0:T(8,128)(2,1)} %param.11), kind=kLoop, calls=%fused_computation.90 | loop fusion | bytes 9437184 | tf_op jit(solution)/shard_map/concatenate | solution.py:46
  31.0 31.1 %all-gather.4.cloned.1.call-done = bf16[1024,6,128]{0,2,1:T(8,128)(2,1)} async-done(((bf16[128,6,128]{0,2,1:T(8,128)(2,1)}), bf16[1024,6,128]{0,2,1:T(8,128)(2,1)}) %all-gather.4.cloned.1.call-update) | async-done | bytes 1572880 | tf_op jit(solution)/shard_map/all_gather | solution.py:49
  62.1 9.5 %fusion.1 = f32[3,3,256,6,128]{2,4,3,1,0:T(8,128)} fusion(bf16[3,3,256,2048]{3,2,1,0:T(8,128)(2,1)} %constant_dynamic-update-slice_fusion, bf16[1024,6,128]{0,2,1:T(8,128)(2,1)} %all-gather.4.cloned.1.call-done), kind=kOutput, calls=%fused_computation.15 | convolution fusion | flops 3623878656 | bytes 13369344 | tf_op jit(solution)/shard_map/pk,krw->prw/dot_general | solution.py:29
  71.6 35.1 %all-gather.6.cloned.1.call-done = bf16[1024,6,128]{0,2,1:T(8,128)(2,1)} async-done(((bf16[128,6,128]{0,2,1:T(8,128)(2,1)}), bf16[1024,6,128]{0,2,1:T(8,128)(2,1)}) %all-gather.6.cloned.1.call-update) | async-done | bytes 1572880 | tf_op jit(solution)/shard_map/all_gather | solution.py:50
  106.8 6.8 %fusion = f32[3,3,256,6,128]{2,4,3,1,0:T(8,128)S(1)} fusion(bf16[3,3,256,2048]{3,2,1,0:T(8,128)(2,1)} %constant_dynamic-update-slice_fusion, bf16[1024,6,128]{0,2,1:T(8,128)(2,1)} %all-gather.6.cloned.1.call-done), kind=kOutput, calls=%fused_computation.13 | convolution fusion | flops 3623878656 | bytes 13369344 | tf_op jit(solution)/shard_map/pk,krw->prw/dot_general | solution.py:29
  113.6 0.0 copy-done
  113.6 0.0 copy-start.3
  113.6 0.8 fusion.12
  114.4 0.0 copy-done.1
  114.4 0.0 copy-done.3
  114.4 0.0 copy-start.2
  114.5 0.1 fusion.23
  114.5 0.7 copy-done.2
  115.3 5.6 %collective-permute-start.2 = (bf16[128,1,128]{0,2,1:T(8,128)(2,1)S(1)}, bf16[128,1,128]{0,2,1:T(8,128)(2,1)S(1)}, u32[]{:S(2)}, u32[]{:S(2)}) collective-permute-start(bf16[128,1,128]{0,2,1:T(8,128)(2,1)S(1)} %get-tuple-element.11), channel_id=1, source_target_pairs={{0,8},{8,16},{16,24},{1,9},{9,17},{17,25},{2,10},{10,18},{18,26},{... | collective-permute-start | bytes 98312 | tf_op jit(solution)/shard_map/ppermute | solution.py:14
  120.9 2.1 %collective-permute-start.3 = (bf16[128,1,128]{0,2,1:T(8,128)(2,1)S(1)}, bf16[128,1,128]{0,2,1:T(8,128)(2,1)S(1)}, u32[]{:S(2)}, u32[]{:S(2)}) collective-permute-start(bf16[128,1,128]{0,2,1:T(8,128)(2,1)S(1)} %get-tuple-element.12), channel_id=1, source_target_pairs={{8,0},{16,8},{24,16},{9,1},{17,9},{25,17},{10,2},{18,10},{26,18},{... | collective-permute-start | bytes 98312 | tf_op jit(solution)/shard_map/ppermute | solution.py:17
  123.0 0.0 collective-permute-done.2
  123.0 3.1 %collective-permute-done.3 = bf16[128,1,128]{0,2,1:T(8,128)(2,1)S(1)} collective-permute-done((bf16[128,1,128]{0,2,1:T(8,128)(2,1)S(1)}, bf16[128,1,128]{0,2,1:T(8,128)(2,1)S(1)}, u32[]{:S(2)}, u32[]{:S(2)}) %collective-permute-start.3) | collective-permute-done | bytes 32800 | tf_op jit(solution)/shard_map/ppermute | solution.py:17
  126.1 0.7 pad_maximum_fusion.1
  126.8 0.0 all-gather.8.cloned.1.call-update
  126.9 0.0 copy-start.6
  126.9 4.4 %fusion.53 = (bf16[3,3,128,1024]{3,2,1,0:T(8,128)(2,1)S(1)}, bf16[3,3,128,1024]{3,2,1,0:T(8,128)(2,1)}) fusion(bf16[3,3,128,2048]{3,2,1,0:T(8,128)(2,1)} %param.12), kind=kLoop, calls=%fused_computation.92 | loop fusion | bytes 9437184 | tf_op jit(solution)/shard_map/slice | solution.py:54
  131.3 0.0 copy-done.6
  131.3 2.2 %convolution_bitcast_fusion.1 = f32[1152,6,128]{0,2,1:T(8,128)S(1)} fusion(bf16[1024,6,128]{0,2,1:T(8,128)(2,1)S(1)} %copy-done.6, bf16[1152,1024,1]{1,0,2:T(8,128)(2,1)S(1)} %bitcast.75), kind=kOutput, calls=%fused_computation.17 | convolution fusion | flops 1811939328 | bytes 7471104 | tf_op jit(solution)/shard_map/pk,krw->prw/dot_general | solution.py:29
  133.5 3.0 %copy.16 = f32[1152,6,128]{2,0,1:T(8,128)} copy(f32[1152,6,128]{0,2,1:T(8,128)S(1)} %convolution_bitcast_fusion.1) | data formatting | bytes 7077888 | tf_op jit(solution)/shard_map/pk,krw->prw/dot_general | solution.py:29
  136.5 3.3 %copy.17 = f32[3,3,128,6,128]{2,4,3,1,0:T(8,128)S(1)} copy(f32[3,3,128,6,128]{4,2,1,0,3:T(8,128)} %bitcast.72) | data formatting | bytes 7077888 | tf_op jit(solution)/shard_map/reshape | solution.py:30
  139.8 26.4 %all-gather.8.cloned.1.call-done = bf16[1024,6,128]{0,2,1:T(8,128)(2,1)} async-done(((bf16[128,6,128]{0,2,1:T(8,128)(2,1)}), bf16[1024,6,128]{0,2,1:T(8,128)(2,1)}) %all-gather.8.cloned.1.call-update) | async-done | bytes 1572880 | tf_op jit(solution)/shard_map/all_gather | solution.py:60
  166.2 6.1 %convolution_bitcast_fusion = f32[1152,6,128]{0,2,1:T(8,128)} fusion(bf16[1024,6,128]{0,2,1:T(8,128)(2,1)} %all-gather.8.cloned.1.call-done, bf16[1152,1024,1]{1,0,2:T(8,128)(2,1)} %bitcast.74), kind=kOutput, calls=%fused_computation.16 | convolution fusion | flops 1811939328 | bytes 7471104 | tf_op jit(solution)/shard_map/pk,krw->prw/dot_general | solution.py:29
  172.4 5.2 %copy.21 = f32[1152,6,128]{2,0,1:T(8,128)} copy(f32[1152,6,128]{0,2,1:T(8,128)} %convolution_bitcast_fusion) | data formatting | bytes 7077888 | tf_op jit(solution)/shard_map/pk,krw->prw/dot_general | solution.py:29
  177.5 0.0 copy-start.4
  177.5 5.2 %copy.22 = f32[3,3,128,6,128]{2,4,3,1,0:T(8,128)} copy(f32[3,3,128,6,128]{4,2,1,0,3:T(8,128)} %bitcast.73) | data formatting | bytes 7077888 | tf_op jit(solution)/shard_map/reshape | solution.py:30
  182.7 0.0 copy-done.4
  182.7 0.0 copy-done.5
  182.7 2.9 %fusion.22 = bf16[128,4,128]{0,2,1:T(8,128)(2,1)} fusion(bf16[128,4,128]{0,2,1:T(8,128)(2,1)} %copy-done.1, f32[1,1,256,4,128]{2,4,3,1,0:T(8,128)} %copy-done.2, f32[3,3,128,6,128]{2,4,3,1,0:T(8,128)} %copy.22, f32[3,3,128,6,128]{2,4,3,1,0:T(8,128)S(1)} %copy.17, f32[128]{0:T(128)S(1)} %copy-done.4, f32[128]{0:T(128)S(1)} %copy-done.5), kind=kLoop, calls=%fused_computation.53 | loop fusion | flops 1835008 | bytes 9176064 | tf_op jit(solution)/shard_map/convert_element_type | solution.py:66
  185.6 1.7 copy.26
  (5 shorter events, 0.1 us)
Async XLA Ops:
  6.5 55.6 %all-gather.4.cloned.1.call-start = ((), (), s32[]{:S(2)}) async-start(), calls=%async_computation | async-start | bytes 1769472 | tf_op jit(solution)/shard_map/all_gather | solution.py:49
  7.6 106.9 %copy-start.1 = (bf16[128,4,128]{0,2,1:T(8,128)(2,1)}, bf16[128,4,128]{0,2,1:T(8,128)(2,1)S(1)}, u32[]{:S(2)}) copy-start(bf16[128,4,128]{0,2,1:T(8,128)(2,1)S(1)} %copy.14) | copy-start | bytes 393220
  8.7 6.5 %collective-permute-start = (bf16[256,1,128]{0,2,1:T(8,128)(2,1)S(1)}, bf16[256,1,128]{0,2,1:T(8,128)(2,1)S(1)}, u32[]{:S(2)}, u32[]{:S(2)}) collective-permute-start(bf16[256,1,128]{0,2,1:T(8,128)(2,1)S(1)} %get-tuple-element.9), channel_id=1, source_target_pairs={{0,8},{8,16},{16,24},{1,9},{9,17},{17,25},{2,10},{10,18},{18,26},{... | collective-permute-start | bytes 196616 | tf_op jit(solution)/shard_map/ppermute | solution.py:14
  13.2 5.6 %collective-permute-start.1 = (bf16[256,1,128]{0,2,1:T(8,128)(2,1)S(1)}, bf16[256,1,128]{0,2,1:T(8,128)(2,1)S(1)}, u32[]{:S(2)}, u32[]{:S(2)}) collective-permute-start(bf16[256,1,128]{0,2,1:T(8,128)(2,1)S(1)} %get-tuple-element.10), channel_id=1, source_target_pairs={{8,0},{16,8},{24,16},{9,1},{17,9},{25,17},{10,2},{18,10},{26,18},{... | collective-permute-start | bytes 196616 | tf_op jit(solution)/shard_map/ppermute | solution.py:17
  19.7 87.0 %all-gather.6.cloned.1.call-start = ((), (), s32[]{:S(2)}) async-start(), calls=%async_computation.1 | async-start | bytes 1769472 | tf_op jit(solution)/shard_map/all_gather | solution.py:50
  20.5 145.7 %all-gather.8.cloned.1.call-start = ((), (), s32[]{:S(2)}) async-start(), calls=%async_computation.2 | async-start | bytes 1769472 | tf_op jit(solution)/shard_map/all_gather | solution.py:60
  106.8 6.8 %copy-start = (f32[3,3,256,6,128]{2,4,3,1,0:T(8,128)S(1)}, f32[3,3,256,6,128]{2,4,3,1,0:T(8,128)}, u32[]{:S(2)}) copy-start(f32[3,3,256,6,128]{2,4,3,1,0:T(8,128)} %fusion.1) | copy-start | bytes 21233668
  113.6 0.8 copy-start.3
  114.4 0.8 copy-start.2
  115.3 7.7 %collective-permute-start.2 = (bf16[128,1,128]{0,2,1:T(8,128)(2,1)S(1)}, bf16[128,1,128]{0,2,1:T(8,128)(2,1)S(1)}, u32[]{:S(2)}, u32[]{:S(2)}) collective-permute-start(bf16[128,1,128]{0,2,1:T(8,128)(2,1)S(1)} %get-tuple-element.11), channel_id=1, source_target_pairs={{0,8},{8,16},{16,24},{1,9},{9,17},{17,25},{2,10},{10,18},{18,26},{... | collective-permute-start | bytes 98312 | tf_op jit(solution)/shard_map/ppermute | solution.py:14
  120.9 5.2 %collective-permute-start.3 = (bf16[128,1,128]{0,2,1:T(8,128)(2,1)S(1)}, bf16[128,1,128]{0,2,1:T(8,128)(2,1)S(1)}, u32[]{:S(2)}, u32[]{:S(2)}) collective-permute-start(bf16[128,1,128]{0,2,1:T(8,128)(2,1)S(1)} %get-tuple-element.12), channel_id=1, source_target_pairs={{8,0},{16,8},{24,16},{9,1},{17,9},{25,17},{10,2},{18,10},{26,18},{... | collective-permute-start | bytes 98312 | tf_op jit(solution)/shard_map/ppermute | solution.py:17
  126.9 4.4 %copy-start.6 = (bf16[1024,6,128]{0,2,1:T(8,128)(2,1)S(1)}, bf16[1024,6,128]{0,2,1:T(8,128)(2,1)}, u32[]{:S(2)}) copy-start(bf16[1024,6,128]{0,2,1:T(8,128)(2,1)} %all-gather.4.cloned.1.call-done) | copy-start | bytes 4718596
  177.5 5.2 %copy-start.4 = (f32[128]{0:T(128)S(1)}, f32[128]{0:T(128)}, u32[]{:S(2)}) copy-start(f32[128]{0:T(128)} %param.15) | copy-start | bytes 1540
  177.5 5.2 %copy-start.5 = (f32[128]{0:T(128)S(1)}, f32[128]{0:T(128)}, u32[]{:S(2)}) copy-start(f32[128]{0:T(128)} %param.13) | copy-start | bytes 1540
Sparse Core Ops, SparseCore 0:
  19.8 42.2 all-gather.3
  64.1 42.5 all-gather.5
  127.0 39.1 all-gather.7
where the time goes:
time: 197 us; the launch traced here: 194 us
  waiting for transfers between devices  100 us (51%)
  local copies, waits for them, and re-layouts  37 us (19%)
  matrix products  24.7 us (13%)
  starting transfers between devices  14.3 us (7%)
  between operations  13.3 us (7%)
  other arithmetic  4.51 us (2%)
    all_gather x1, waiting for transfers between devices, per_device(): h_piece = lax.all_gather(padded[in_dev:], 'chan', axis=0, tiled=True)  35.1 us
    all_gather x1, waiting for transfers between devices, per_device(): x_piece = lax.all_gather(padded[:in_dev], 'chan', axis=0, tiled=True)  31.1 us
    all_gather x1, waiting for transfers between devices, per_device(): piece = lax.all_gather(reset_rows, 'chan', axis=0, tiled=True)  26.4 us
    dot_general x4, matrix products, conv_rows(): jnp.einsum('pk,krw->prw', flat, source, preferred_element_type=jnp.float32)  24.7 us
    ppermute x2, starting transfers between devices, extended(): lax.ppermute(lax.slice_in_dim(block, block.shape[dim] - width, None, axis...  10.1 us
    reshape x2, local copies, waits for them, and re-layouts, conv_rows(): product = product.reshape(3, 3, outputs, src_rows, out_cols)  8.52 us
    dot_general x2, local copies, waits for them, and re-layouts, conv_rows(): jnp.einsum('pk,krw->prw', flat, source, preferred_element_type=jnp.float32)  8.15 us
    unnamed x17, local copies, waits for them, and re-layouts  8.1 us
  transfers between devices with their start and end apart: 7, of which 5 were waited for; matrix products, arithmetic and copies ran while one was open for 17% of the time, Pallas kernels for 0%

commit v1 on v0

v1 whole, which is shorter than its diff:
```python
import functools

import jax
import jax.numpy as jnp
from jax import lax
from jax.experimental import pallas as pl
from jax.experimental.pallas import tpu as pltpu
from jax.sharding import PartitionSpec as P

MESH = pl.DeviceIdType.MESH
PAIR = 2


def kernel(
    n_chan, n_rows, cols,
    loc, bias, w_update, w_reset, w_cand,
    out,
    joined, rh, rh_loc, weights, acc, acc_cand, gate,
    w_sem, own_sem, send1, band1, rim1, send2, band2, rim2,
):
    n = loc.shape[1]
    band = loc.shape[2]
    channels = joined.shape[1]
    lines = n_chan // PAIR
    me = lax.axis_index("chan")
    row = lax.axis_index("rows")
    line, pair = me // PAIR, me % PAIR
    has_up, has_down = line < lines - 1, line > 0
    has_above, has_below = row > 0, row < n_rows - 1

    w_copies = [
        pltpu.make_async_copy(src, weights.at[i], w_sem.at[i])
        for i, src in enumerate((w_reset, w_update, w_cand))
    ]
    for copy in w_copies:
        copy.start()

    def ident(l, p):
        return l * PAIR + p

    up, down, partner = ident(line + 1, pair), ident(line - 1, pair), ident(line, 1 - pair)
    barrier = pltpu.get_barrier_semaphore()

    def greet(there, target):
        @pl.when(there)
        def _():
            pl.semaphore_signal(barrier, inc=1, device_id=target, device_id_type=MESH)

    pl.semaphore_signal(barrier, inc=1, device_id={"chan": partner}, device_id_type=MESH)
    greet(has_up, {"chan": up})
    greet(has_down, {"chan": down})
    greet(has_above, {"rows": row - 1})
    greet(has_below, {"rows": row + 1})
    pl.semaphore_wait(
        barrier,
        1
        + has_up.astype(jnp.int32)
        + has_down.astype(jnp.int32)
        + has_above.astype(jnp.int32)
        + has_below.astype(jnp.int32),
    )

    def mover(own, buf, send, band_sem, rim_sem):
        def place(c):
            return pl.ds(pl.multiple_of(c * n, n), n)

        def band_copy(kind, c, mine, target):
            dst = buf.at[:, place(c), pl.ds(cols, band)]
            return pltpu.make_async_remote_copy(
                src_ref=own if mine else dst,
                dst_ref=dst,
                send_sem=send.at[kind, c],
                recv_sem=band_sem.at[c],
                device_id={"chan": target},
                device_id_type=MESH,
            )

        def rim_copy(side, c, mine):
            start = 0 if side == 0 else band - cols
            src = (
                own.at[:, :, pl.ds(start, cols)]
                if mine
                else buf.at[:, place(c), pl.ds(cols + start, cols)]
            )
            dst_col = cols + band if side == 0 else 0
            return pltpu.make_async_remote_copy(
                src_ref=src,
                dst_ref=buf.at[:, place(c), pl.ds(dst_col, cols)],
                send_sem=send.at[3 + side, c],
                recv_sem=rim_sem.at[side, c],
                device_id={"rows": row - 1 if side == 0 else row + 1},
                device_id_type=MESH,
            )

        def rims(c, mine, act):
            @pl.when(has_above)
            def _():
                act(rim_copy(0, c, mine))

            @pl.when(has_below)
            def _():
                act(rim_copy(1, c, mine))

        def start(copy):
            copy.start()

        def done(copy):
            copy.wait_send()

        def send_up(c, mine, act):
            @pl.when(has_up)
            def _():
                act(band_copy(0, c, mine, up))

        def send_down(c, mine, act):
            @pl.when(has_down)
            def _():
                act(band_copy(1, c, mine, down))

        def local():
            return pltpu.make_async_copy(
                own, buf.at[:, place(me), pl.ds(cols, band)], own_sem
            )

        def begin(act):
            band_copy(2, me, True, partner).start() if act is start else band_copy(
                2, me, True, partner
            ).wait_send()
            send_up(me, True, act)
            send_down(me, True, act)
            rims(me, True, act)

        def from_below(s, act, first):
            c = ident(line - s, pair)

            @pl.when(line >= s)
            def _():
                if first:
                    band_copy(0, c, False, partner).wait_recv()
                act(band_copy(2, c, False, partner))
                send_up(c, False, act)
                rims(c, False, act)

        def from_above(s, act, first):
            c = ident(line + s, pair)

            @pl.when(line + s < lines)
            def _():
                if first:
                    band_copy(0, c, False, partner).wait_recv()
                act(band_copy(2, c, False, partner))
                send_down(c, False, act)
                rims(c, False, act)

        def from_pair(l, ok, act, first):
            c = ident(l, 1 - pair)

            @pl.when(ok)
            def _():
                if first:
                    band_copy(2, c, False, partner).wait_recv()
                rims(c, False, act)

        def ready(c):
            @pl.when(has_below)
            def _():
                rim_copy(0, c, False).wait_recv()

            @pl.when(has_above)
            def _():
                rim_copy(1, c, False).wait_recv()

        def across(s, act, first):
            from_pair(line - s, line >= s, act, first)
            if s > 0:
                from_pair(line + s, line + s < lines, act, first)

        def run(compute):
            eager = n % 128 == 0

            def use(s, p):
                if not eager:
                    return
                for l, ok in (
                    (line - s, line >= s),
                    (line + s, line + s < lines),
                )[: 1 if s == 0 else 2]:
                    @pl.when(ok)
                    def _():
                        c = ident(l, p)
                        ready(c)
                        compute(c)

            local().wait()
            for s in range(1, lines):
                from_below(s, start, True)
                from_above(s, start, True)
                across(s - 1, start, True)
                use(s - 1, pair)
                if s >= 2:
                    use(s - 2, 1 - pair)
            across(lines - 1, start, True)
            if lines >= 2:
                use(lines - 2, 1 - pair)
            use(lines - 1, pair)
            use(lines - 1, 1 - pair)
            if not eager:
                for c in range(n_chan):
                    ready(c)
                for g in range(channels // 128):
                    compute(g)

        def finish():
            begin(done)
            for s in range(1, lines):
                from_below(s, done, False)
                from_above(s, done, False)
            for s in range(lines):
                across(s, done, False)

        def launch():
            begin(start)
            local().start()

        return launch, run, finish

    launch1, run1, finish1 = mover(loc, joined, send1, band1, rim1)
    launch2, run2, finish2 = mover(rh_loc, rh, send2, band2, rim2)
    launch1()

    @pl.when(jnp.logical_not(has_above))
    def _():
        for buf in (joined, rh):
            buf[:, :, pl.ds(0, cols)] = jnp.zeros((buf.shape[0], channels, cols), buf.dtype)

    @pl.when(jnp.logical_not(has_below))
    def _():
        for buf in (joined, rh):
            buf[:, :, pl.ds(cols + band, cols)] = jnp.zeros(
                (buf.shape[0], channels, cols), buf.dtype
            )

    def part(gates, parts, ks_list, buf, bufs, g):
        ks = pl.ds(pl.multiple_of(g * 128, 128), 128)
        left, right = [], []
        for a in range(3):
            for offset, b in zip(ks_list, bufs):
                kw = pl.ds(pl.multiple_of(offset + g * 128, 128), 128)
                w = weights[pl.ds(gates, parts), a, :, :, kw]
                left.append(w.reshape(parts * 3 * n, 128))
                right.append(buf[b, ks, pl.ds(a * cols, band)])
        return jnp.dot(
            jnp.concatenate(left, 1),
            jnp.concatenate(right, 0),
            preferred_element_type=jnp.float32,
        )

    acc[...] = jnp.zeros_like(acc)
    for copy in w_copies:
        copy.wait()

    def gates_on(g):
        for i in range(2):
            acc[i] += part(i, 1, (0, channels), joined, (0, 1), g)

    run1(gates_on)

    lane = lax.broadcasted_iota(jnp.int32, (n, cols), 1)

    def folded(ref, i, r):
        cells = pl.ds(r * cols, cols)
        low = pltpu.roll(ref[i, pl.ds(0, n), cells], 1, 1)
        mid = ref[i, pl.ds(n, n), cells]
        high = pltpu.roll(ref[i, pl.ds(2 * n, n), cells], cols - 1, 1)
        return jnp.where(lane == 0, 0.0, low) + mid + jnp.where(lane == cols - 1, 0.0, high)

    for r in range(band // cols):
        cells = pl.ds(r * cols, cols)
        reset = jax.nn.sigmoid(folded(acc, 0, r) + bias[1])
        rh_loc[0, :, cells] = (reset * loc[1, :, cells].astype(jnp.float32)).astype(rh_loc.dtype)
    launch2()

    for r in range(band // cols):
        gate[:, pl.ds(r * cols, cols)] = jax.nn.sigmoid(folded(acc, 1, r) + bias[0])
    acc_cand[0] = part(2, 1, (0,), joined, (0,), 0)

    @pl.loop(1, channels // 128)
    def _(g):
        acc_cand[0] += part(2, 1, (0,), joined, (0,), g)

    def cand_on(g):
        acc_cand[0] += part(2, 1, (channels,), rh, (0,), g)

    run2(cand_on)

    for r in range(band // cols):
        cells = pl.ds(r * cols, cols)
        candidate = jnp.tanh(folded(acc_cand, 0, r) + bias[2])
        update = gate[:, cells]
        out[:, cells] = (
            (1.0 - update) * loc[1, :, cells].astype(jnp.float32) + update * candidate
        ).astype(out.dtype)
    finish1()
    finish2()


def per_device(n_chan, n_rows, features, hidden, w_update, w_reset, w_cand, b_update, b_reset, b_cand):
    n, rows, cols = features.shape
    band = rows * cols
    channels = n * n_chan
    wide = band + 2 * cols
    loc = jnp.stack([features.reshape(n, band), hidden.reshape(n, band)])
    bias = jnp.stack([b_update, b_reset, b_cand])[:, :, None]
    bf16, f32 = jnp.bfloat16, jnp.float32
    vmem = pl.BlockSpec(memory_space=pltpu.VMEM)
    hbm = pl.BlockSpec(memory_space=pl.ANY)
    dma = pltpu.SemaphoreType.DMA
    result = pl.pallas_call(
        functools.partial(kernel, n_chan, n_rows, cols),
        out_shape=jax.ShapeDtypeStruct((n, band), bf16),
        in_specs=[vmem, vmem, hbm, hbm, hbm],
        out_specs=vmem,
        scratch_shapes=[
            pltpu.VMEM((2, channels, wide), bf16),
            pltpu.VMEM((1, channels, wide), bf16),
            pltpu.VMEM((1, n, band), bf16),
            pltpu.VMEM((3,) + w_update.shape, bf16),
            pltpu.VMEM((2, 3 * n, band), f32),
            pltpu.VMEM((1, 3 * n, band), f32),
            pltpu.VMEM((n, band), f32),
            dma((3,)),
            dma,
            dma((5, n_chan)),
            dma((n_chan,)),
            dma((2, n_chan)),
            dma((5, n_chan)),
            dma((n_chan,)),
            dma((2, n_chan)),
        ],
        compiler_params=pltpu.CompilerParams(
            collective_id=0, has_side_effects=True, vmem_limit_bytes=60 * 1024 * 1024
        ),
    )(loc, bias, w_update, w_reset, w_cand)
    return result.reshape(n, rows, cols)


def solution(mesh):
    in_specs = (
        P("chan", "rows", None),
        P("chan", "rows", None),
        P(None, None, "chan", None),
        P(None, None, "chan", None),
        P(None, None, "chan", None),
        P("chan"),
        P("chan"),
        P("chan"),
    )
    return jax.shard_map(
        functools.partial(per_device, mesh.shape["chan"], mesh.shape["rows"]),
        mesh=mesh,
        in_specs=in_specs,
        out_specs=P("chan", "rows", None),
        check_vma=False,
    )
```

time: 197 us -> 61.6 us (0.31); the launches traced: 194 us -> 61.3 us
  waiting for transfers between devices: 100 us -> 0 us
  Pallas kernels: 0 us -> 55.6 us
  local copies, waits for them, and re-layouts: 37 us -> 4.35 us
  matrix products: 24.7 us -> 0 us
  starting transfers between devices: 14.3 us -> 0 us
  between operations: 13.3 us -> 0.02 us
  other arithmetic: 4.51 us -> 1.41 us
    all_gather x3 -> x0, waiting for transfers between devices: 92.6 us -> none  [the longest x1 35.1 us: per_device(): h_piece = lax.all_gather(padded[in_dev:], 'chan', axis=0, tiled=True)]
    pallas_call x0 -> x1, Pallas kernels: none -> 55.6 us  [per_device(): pl.pallas_call(functools.partial(kernel, n_chan, n_rows, cols), out_shape...]
    dot_general x4 -> x0, matrix products: 24.7 us -> none  [conv_rows(): jnp.einsum('pk,krw->prw', flat, source, preferred_element_type=jnp.float32)]
    ppermute x4 -> x0, starting transfers between devices: 14.2 us -> none  [the longest x2 10.1 us: extended(): lax.ppermute(lax.slice_in_dim(block, block.shape[dim] - width, None, axis...]
    dot_general x2 -> x0, local copies, waits for them, and re-layouts: 8.15 us -> none  [conv_rows(): jnp.einsum('pk,krw->prw', flat, source, preferred_element_type=jnp.float32)]
    unnamed x17 -> x0, local copies, waits for them, and re-layouts: 8.1 us -> none
    reshape x2 -> x1, local copies, waits for them, and re-layouts: 8.52 us -> 1.59 us  [per_device(): return result.reshape(n, rows, cols)]
    ppermute x4 -> x0, waiting for transfers between devices: 6.77 us -> none  [the longest x2 6.76 us: extended(): lax.ppermute(lax.slice_in_dim(block, 0, width, axis=dim), axis, backward)]
  transfers between devices with their start and end apart: 7 -> 0, of which waited for: 5 -> 0; matrix products, arithmetic and copies ran while one was open for 17% -> 0% of each run, Pallas kernels for 0% -> 0%
where the time goes in v1:
time: 61.6 us; the launch traced here: 61.3 us
  Pallas kernels  55.6 us (90%)
  local copies, waits for them, and re-layouts  4.35 us (7%)
  other arithmetic  1.41 us (2%)
    pallas_call x1, Pallas kernels, per_device(): pl.pallas_call(functools.partial(kernel, n_chan, n_rows, cols), out_shape...  55.6 us
    another operation x2, local copies, waits for them, and re-layouts, per_device(): loc = jnp.stack([features.reshape(n, band), hidden.reshape(n, band)])  1.92 us
    reshape x1, local copies, waits for them, and re-layouts, per_device(): return result.reshape(n, rows, cols)  1.59 us

profile of v1, /device:TPU:1, one launch (start us, length us, event | category | flops | bytes accessed | tf_op | source)
XLA Modules:
  0.0 61.3 jit_solution(1064486316344015085)
XLA Ops:
  0.0 0.7 %maximum_bitcast_fusion = f32[3,128,1]{1,0,2:T(4,128)S(1)} fusion(f32[1,128]{1,0:T(1,128)} %bitcast.5, f32[1,128]{1,0:T(1,128)} %bitcast.6, f32[1,128]{1,0:T(1,128)} %bitcast.7), kind=kLoop, calls=%fused_computation.1 | loop fusion | flops 768 | bytes 3072 | tf_op jit(solution)/shard_map/broadcast_in_dim | solution.py:313
  0.7 1.0 %stack_reshape.6 = bf16[1,128,512]{2,1,0:T(8,128)(2,1)S(1)} reshape(bf16[128,4,128]{2,1,0:T(4,128)(2,1)} %param.8) | data formatting | bytes 262144 | tf_op jit(solution)/shard_map/stack;reshape | solution.py:312
  1.7 1.0 %stack_reshape.7 = bf16[1,128,512]{2,1,0:T(8,128)(2,1)S(1)} reshape(bf16[128,4,128]{2,1,0:T(4,128)(2,1)} %param.9) | data formatting | bytes 262144 | tf_op jit(solution)/shard_map/stack;reshape | solution.py:312
  2.6 0.7 %pad_maximum_fusion.loc = bf16[2,128,512]{2,1,0:T(8,128)(2,1)} fusion(bf16[1,128,512]{2,1,0:T(8,128)(2,1)S(1)} %stack_reshape.7, bf16[1,128,512]{2,1,0:T(8,128)(2,1)S(1)} %stack_reshape.6), kind=kLoop, calls=%fused_computation | loop fusion | flops 131072 | bytes 524288 | tf_op jit(solution)/shard_map/stack | solution.py:312
  3.3 0.8 %copy.9.bias = f32[3,128,1]{2,1,0:T(8,128)} copy(f32[3,128,1]{1,0,2:T(4,128)S(1)} %maximum_bitcast_fusion) | data formatting | bytes 3072 | tf_op jit(solution)/shard_map/broadcast_in_dim | solution.py:313
  4.2 55.6 %shard_map.82 = bf16[128,512]{1,0:T(8,128)(2,1)} custom-call(bf16[2,128,512]{2,1,0:T(8,128)(2,1)} %pad_maximum_fusion.loc, f32[3,128,1]{2,1,0:T(8,128)} %copy.9.bias, bf16[3,3,128,2048]{3,2,1,0:T(8,128)(2,1)} %w_update.1, bf16[3,3,128,2048]{3,2,1,0:T(8,128)(2,1)} %w_reset.1, bf16[3,3,128,2048]{3,2,1,0:T(8,128)(2,1)} %w_cand.1), custom_call_target="tpu_custom_call" | custom-call | tf_op jit(solution)/shard_map/pallas_call | solution.py:318
  59.7 1.6 %reshape.3 = bf16[128,4,128]{2,1,0:T(4,128)(2,1)} reshape(bf16[128,512]{1,0:T(8,128)(2,1)} %shard_map.82) | data formatting | bytes 262144 | tf_op jit(solution)/shard_map/reshape | solution.py:344

commit v2 on v1

v2 whole, which is shorter than its diff:
```python
import functools

import jax
import jax.numpy as jnp
from jax import lax
from jax.experimental import pallas as pl
from jax.experimental.pallas import tpu as pltpu
from jax.sharding import PartitionSpec as P

MESH = pl.DeviceIdType.MESH
PAIR = 2


def kernel(
    n_chan, n_rows, cols,
    features, hidden, b_update, b_reset, b_cand, w_update, w_reset, w_cand,
    out,
    joined, rh, rh_loc, weights, acc, acc_cand, gate,
    w_sem, own_sem, send1, band1, rim1, send2, band2, rim2,
):
    n = features.shape[0]
    band = features.shape[1]
    channels = joined.shape[1]
    lines = n_chan // PAIR
    me = lax.axis_index("chan")
    row = lax.axis_index("rows")
    line, pair = me // PAIR, me % PAIR
    has_up, has_down = line < lines - 1, line > 0
    has_above, has_below = row > 0, row < n_rows - 1

    w_copies = [
        pltpu.make_async_copy(src, weights.at[i], w_sem.at[i])
        for i, src in enumerate((w_reset, w_update, w_cand))
    ]
    for copy in w_copies:
        copy.start()

    def ident(l, p):
        return l * PAIR + p

    up, down, partner = ident(line + 1, pair), ident(line - 1, pair), ident(line, 1 - pair)
    barrier = pltpu.get_barrier_semaphore()

    def greet(there, target):
        @pl.when(there)
        def _():
            pl.semaphore_signal(barrier, inc=1, device_id=target, device_id_type=MESH)

    pl.semaphore_signal(barrier, inc=1, device_id={"chan": partner}, device_id_type=MESH)
    greet(has_up, {"chan": up})
    greet(has_down, {"chan": down})
    greet(has_above, {"rows": row - 1})
    greet(has_below, {"rows": row + 1})
    pl.semaphore_wait(
        barrier,
        1
        + has_up.astype(jnp.int32)
        + has_down.astype(jnp.int32)
        + has_above.astype(jnp.int32)
        + has_below.astype(jnp.int32),
    )

    def mover(own, dest, own_sem, send, band_sem, rim_sem):
        def band_copy(kind, c, h, mine, target):
            dst = dest(c, h, cols, band)
            return pltpu.make_async_remote_copy(
                src_ref=own(h, 0, band) if mine else dst,
                dst_ref=dst,
                send_sem=send.at[kind, c, h],
                recv_sem=band_sem.at[c, h],
                device_id={"chan": target},
                device_id_type=MESH,
            )

        def rim_copy(side, c, h, mine):
            first = 0 if side == 0 else band - cols
            return pltpu.make_async_remote_copy(
                src_ref=own(h, first, cols) if mine else dest(c, h, cols + first, cols),
                dst_ref=dest(c, h, cols + band if side == 0 else 0, cols),
                send_sem=send.at[3 + side, c, h],
                recv_sem=rim_sem.at[side, c, h],
                device_id={"rows": row - 1 if side == 0 else row + 1},
                device_id_type=MESH,
            )

        def start(copy):
            copy.start()

        def done(copy):
            copy.wait_send()

        def rims(c, h, mine, act):
            @pl.when(has_above)
            def _():
                act(rim_copy(0, c, h, mine))

            @pl.when(has_below)
            def _():
                act(rim_copy(1, c, h, mine))

        def send_line(kind, ok, c, h, mine, act):
            @pl.when(ok)
            def _():
                act(band_copy(kind, c, h, mine, up if kind == 0 else down))

        def local(h):
            return pltpu.make_async_copy(own(h, 0, band), dest(me, h, cols, band), own_sem.at[h])

        def begin(act):
            for h in range(2):
                send_line(0, has_up, me, h, True, act)
                send_line(1, has_down, me, h, True, act)
                act(band_copy(2, me, h, True, partner))
            for h in range(2):
                rims(me, h, True, act)

        def from_below(s, h, act, first):
            c = ident(line - s, pair)

            @pl.when(line >= s)
            def _():
                if first:
                    band_copy(0, c, h, False, partner).wait_recv()
                send_line(0, has_up, c, h, False, act)
                act(band_copy(2, c, h, False, partner))
                rims(c, h, False, act)

        def from_above(s, h, act, first):
            c = ident(line + s, pair)

            @pl.when(line + s < lines)
            def _():
                if first:
                    band_copy(0, c, h, False, partner).wait_recv()
                send_line(1, has_down, c, h, False, act)
                act(band_copy(2, c, h, False, partner))
                rims(c, h, False, act)

        def from_pair(l, ok, act, first):
            c = ident(l, 1 - pair)

            @pl.when(ok)
            def _():
                for h in range(2):
                    if first:
                        band_copy(2, c, h, False, partner).wait_recv()
                    rims(c, h, False, act)

        def ready(c):
            for h in range(2):
                @pl.when(has_below)
                def _():
                    rim_copy(0, c, h, False).wait_recv()

                @pl.when(has_above)
                def _():
                    rim_copy(1, c, h, False).wait_recv()

        def across(s, act, first):
            from_pair(line - s, line >= s, act, first)
            if s > 0:
                from_pair(line + s, line + s < lines, act, first)

        def run(compute):
            eager = n % 128 == 0

            def use(s, p):
                if not eager:
                    return
                for l, ok in (
                    (line - s, line >= s),
                    (line + s, line + s < lines),
                )[: 1 if s == 0 else 2]:
                    @pl.when(ok)
                    def _():
                        c = ident(l, p)
                        ready(c)
                        compute(c)

            for h in range(2):
                local(h).wait()
            for s in range(1, lines):
                for h in range(2):
                    from_below(s, h, start, True)
                    from_above(s, h, start, True)
                across(s - 1, start, True)
                use(s - 1, pair)
                if s >= 2:
                    use(s - 2, 1 - pair)
            if lines >= 2:
                use(lines - 2, 1 - pair)
            use(lines - 1, pair)
            across(lines - 1, start, True)
            use(lines - 1, 1 - pair)
            if not eager:
                for c in range(n_chan):
                    ready(c)
                for g in range(channels // 128):
                    compute(g)

        def finish():
            begin(done)
            for s in range(1, lines):
                for h in range(2):
                    from_below(s, h, done, False)
                    from_above(s, h, done, False)
            for s in range(lines):
                across(s, done, False)

        def launch():
            begin(start)
            for h in range(2):
                local(h).start()

        return launch, run, finish

    def own1(h, start, size):
        return (features, hidden)[h].at[:, pl.ds(start, size)]

    def dest1(c, h, start, size):
        return joined.at[h, pl.ds(pl.multiple_of(c * n, n), n), pl.ds(start, size)]

    half = n // 2

    def own2(h, start, size):
        return rh_loc.at[pl.ds(h * half, half), pl.ds(start, size)]

    def dest2(c, h, start, size):
        return rh.at[
            0, pl.ds(pl.multiple_of(c * n + h * half, half), half), pl.ds(start, size)
        ]

    launch1, run1, finish1 = mover(own1, dest1, own_sem.at[0], send1, band1, rim1)
    launch2, run2, finish2 = mover(own2, dest2, own_sem.at[1], send2, band2, rim2)
    launch1()

    @pl.when(jnp.logical_not(has_above))
    def _():
        for buf in (joined, rh):
            buf[:, :, pl.ds(0, cols)] = jnp.zeros((buf.shape[0], channels, cols), buf.dtype)

    @pl.when(jnp.logical_not(has_below))
    def _():
        for buf in (joined, rh):
            buf[:, :, pl.ds(cols + band, cols)] = jnp.zeros(
                (buf.shape[0], channels, cols), buf.dtype
            )

    def part(gates, parts, ks_list, buf, bufs, g):
        ks = pl.ds(pl.multiple_of(g * 128, 128), 128)
        left, right = [], []
        for a in range(3):
            for offset, b in zip(ks_list, bufs):
                kw = pl.ds(pl.multiple_of(offset + g * 128, 128), 128)
                w = weights[pl.ds(gates, parts), a, :, :, kw]
                left.append(w.reshape(parts * 3 * n, 128))
                right.append(buf[b, ks, pl.ds(a * cols, band)])
        return jnp.dot(
            jnp.concatenate(left, 1),
            jnp.concatenate(right, 0),
            preferred_element_type=jnp.float32,
        )

    acc[...] = jnp.zeros_like(acc)
    for copy in w_copies:
        copy.wait()

    def gates_on(g):
        for i in range(2):
            acc[i] += part(i, 1, (0, channels), joined, (0, 1), g)

    run1(gates_on)

    lane = lax.broadcasted_iota(jnp.int32, (n, cols), 1)

    diagonal = lax.broadcasted_iota(jnp.int32, (n, n), 0) == lax.broadcasted_iota(
        jnp.int32, (n, n), 1
    )

    def column(ref):
        return jnp.sum(jnp.where(diagonal, ref[...], 0.0), axis=1, keepdims=True)

    def folded(ref, i, r):
        cells = pl.ds(r * cols, cols)
        low = pltpu.roll(ref[i, pl.ds(0, n), cells], 1, 1)
        mid = ref[i, pl.ds(n, n), cells]
        high = pltpu.roll(ref[i, pl.ds(2 * n, n), cells], cols - 1, 1)
        return jnp.where(lane == 0, 0.0, low) + mid + jnp.where(lane == cols - 1, 0.0, high)

    for r in range(band // cols):
        cells = pl.ds(r * cols, cols)
        reset = jax.nn.sigmoid(folded(acc, 0, r) + column(b_reset))
        rh_loc[:, cells] = (reset * hidden[:, cells].astype(jnp.float32)).astype(rh_loc.dtype)
    launch2()

    for r in range(band // cols):
        gate[:, pl.ds(r * cols, cols)] = jax.nn.sigmoid(folded(acc, 1, r) + column(b_update))
    acc_cand[0] = part(2, 1, (0,), joined, (0,), 0)

    @pl.loop(1, channels // 128)
    def _(g):
        acc_cand[0] += part(2, 1, (0,), joined, (0,), g)

    def cand_on(g):
        acc_cand[0] += part(2, 1, (channels,), rh, (0,), g)

    run2(cand_on)

    for r in range(band // cols):
        cells = pl.ds(r * cols, cols)
        candidate = jnp.tanh(folded(acc_cand, 0, r) + column(b_cand))
        update = gate[:, cells]
        out[:, cells] = (
            (1.0 - update) * hidden[:, cells].astype(jnp.float32) + update * candidate
        ).astype(out.dtype)
    finish1()
    finish2()


def per_device(n_chan, n_rows, features, hidden, w_update, w_reset, w_cand, b_update, b_reset, b_cand):
    n, rows, cols = features.shape
    band = rows * cols
    channels = n * n_chan
    wide = band + 2 * cols
    bf16, f32 = jnp.bfloat16, jnp.float32
    vmem = pl.BlockSpec(memory_space=pltpu.VMEM)
    hbm = pl.BlockSpec(memory_space=pl.ANY)
    dma = pltpu.SemaphoreType.DMA
    result = pl.pallas_call(
        functools.partial(kernel, n_chan, n_rows, cols),
        out_shape=jax.ShapeDtypeStruct((n, band), bf16),
        in_specs=[vmem] * 5 + [hbm] * 3,
        out_specs=vmem,
        scratch_shapes=[
            pltpu.VMEM((2, channels, wide), bf16),
            pltpu.VMEM((1, channels, wide), bf16),
            pltpu.VMEM((n, band), bf16),
            pltpu.VMEM((3,) + w_update.shape, bf16),
            pltpu.VMEM((2, 3 * n, band), f32),
            pltpu.VMEM((1, 3 * n, band), f32),
            pltpu.VMEM((n, band), f32),
            dma((3,)),
            dma((2, 2)),
            dma((5, n_chan, 2)),
            dma((n_chan, 2)),
            dma((2, n_chan, 2)),
            dma((5, n_chan, 2)),
            dma((n_chan, 2)),
            dma((2, n_chan, 2)),
        ],
        compiler_params=pltpu.CompilerParams(
            collective_id=0, has_side_effects=True, vmem_limit_bytes=60 * 1024 * 1024
        ),
    )(
        features.reshape(n, band),
        hidden.reshape(n, band),
        b_update.reshape(1, n),
        b_reset.reshape(1, n),
        b_cand.reshape(1, n),
        w_update,
        w_reset,
        w_cand,
    )
    return result.reshape(n, rows, cols)


def solution(mesh):
    in_specs = (
        P("chan", "rows", None),
        P("chan", "rows", None),
        P(None, None, "chan", None),
        P(None, None, "chan", None),
        P(None, None, "chan", None),
        P("chan"),
        P("chan"),
        P("chan"),
    )
    return jax.shard_map(
        functools.partial(per_device, mesh.shape["chan"], mesh.shape["rows"]),
        mesh=mesh,
        in_specs=in_specs,
        out_specs=P("chan", "rows", None),
        check_vma=False,
    )
```

time: 61.6 us -> 57.2 us (0.929)
  Pallas kernels: 55.6 us -> 53.7 us
  other arithmetic: 1.41 us -> 0 us
  local copies, waits for them, and re-layouts: 4.35 us -> 3.28 us
    another operation x2 -> x0, local copies, waits for them, and re-layouts: 1.92 us -> none  [per_device(): loc = jnp.stack([features.reshape(n, band), hidden.reshape(n, band)])]
    pallas_call x1, Pallas kernels: 55.6 us -> 53.7 us  [per_device(): pl.pallas_call(functools.partial(kernel, n_chan, n_rows, cols), out_shape...]
    reshape x0 -> x1, local copies, waits for them, and re-layouts: none -> 1.69 us  [per_device(): hidden.reshape(n, band)]
    broadcast_in_dim x1 -> x0, local copies, waits for them, and re-layouts: 0.83 us -> none  [per_device(): bias = jnp.stack([b_update, b_reset, b_cand])[:, :, None]]
    another operation x1 -> x0, other arithmetic: 0.72 us -> none  [per_device(): loc = jnp.stack([features.reshape(n, band), hidden.reshape(n, band)])]
    broadcast_in_dim x1 -> x0, other arithmetic: 0.7 us -> none  [per_device(): bias = jnp.stack([b_update, b_reset, b_cand])[:, :, None]]
where the time goes in v2:
time: 57.2 us; the launch traced here: 57 us
  Pallas kernels  53.7 us (94%)
  local copies, waits for them, and re-layouts  3.28 us (6%)
    pallas_call x1, Pallas kernels, per_device(): pl.pallas_call(functools.partial(kernel, n_chan, n_rows, cols), out_shape...  53.7 us
    reshape x1, local copies, waits for them, and re-layouts, per_device(): hidden.reshape(n, band)  1.69 us
    reshape x1, local copies, waits for them, and re-layouts, per_device(): return result.reshape(n, rows, cols)  1.59 us

profile of v2, /device:TPU:1, one launch (start us, length us, event | category | flops | bytes accessed | tf_op | source)
XLA Modules:
  0.0 57.0 jit_solution(16717736282393652343)
XLA Ops:
  0.0 1.7 %copy_bitcast_fusion = (bf16[128,512]{1,0:T(8,128)(2,1)}, bf16[128,512]{1,0:T(8,128)(2,1)}) fusion(bf16[16,8,4,128]{3,2,1,0:T(4,128)(2,1)} %bitcast.9, bf16[16,8,4,128]{3,2,1,0:T(4,128)(2,1)} %bitcast.10), kind=kLoop, calls=%fused_computation | loop fusion | bytes 524288 | tf_op jit(solution)/shard_map/reshape | solution.py:356
  1.7 53.7 %shard_map.82 = bf16[128,512]{1,0:T(8,128)(2,1)} custom-call(bf16[128,512]{1,0:T(8,128)(2,1)} %get-tuple-element.6.features, bf16[128,512]{1,0:T(8,128)(2,1)} %get-tuple-element.5.hidden, f32[1,128]{1,0:T(1,128)} %bitcast.11, f32[1,128]{1,0:T(1,128)} %bitcast.12, f32[1,128]{1,0:T(1,128)} %bitcast.13, bf16[3,3,128,2048]{3,2,1,0:T(8,128)(2,1)} %w_update.1, ...), custom_call_target="tpu_custom_call" | custom-call | tf_op jit(solution)/shard_map/pallas_call | solution.py:329
  55.4 1.6 %reshape.23 = bf16[128,4,128]{2,1,0:T(4,128)(2,1)} reshape(bf16[128,512]{1,0:T(8,128)(2,1)} %shard_map.82) | data formatting | bytes 262144 | tf_op jit(solution)/shard_map/reshape | solution.py:364

commit v3 on v2

--- a/solution.py
+++ b/solution.py
@@ -180,10 +180,11 @@
             for h in range(2):
                 local(h).wait()
             for s in range(1, lines):
-                for h in range(2):
-                    from_below(s, h, start, True)
-                    from_above(s, h, start, True)
+                from_below(s, 0, start, True)
+                from_above(s, 0, start, True)
                 across(s - 1, start, True)
+                from_below(s, 1, start, True)
+                from_above(s, 1, start, True)
                 use(s - 1, pair)
                 if s >= 2:
                     use(s - 2, 1 - pair)

time: 57.2 us -> 62.6 us (1.094)
  Pallas kernels: 53.7 us -> 59.1 us
    pallas_call x1, Pallas kernels: 53.7 us -> 59.1 us  [per_device(): pl.pallas_call(functools.partial(kernel, n_chan, n_rows, cols), out_shape...]
where the time goes in v3:
time: 62.6 us; the launch traced here: 62.4 us
  Pallas kernels  59.1 us (94%)
  local copies, waits for them, and re-layouts  3.28 us (5%)
    pallas_call x1, Pallas kernels, per_device(): pl.pallas_call(functools.partial(kernel, n_chan, n_rows, cols), out_shape...  59.1 us
    reshape x1, local copies, waits for them, and re-layouts, per_device(): hidden.reshape(n, band)  1.69 us
    reshape x1, local copies, waits for them, and re-layouts, per_device(): return result.reshape(n, rows, cols)  1.59 us

profile of v3, /device:TPU:1, one launch (start us, length us, event | category | flops | bytes accessed | tf_op | source)
XLA Modules:
  0.0 62.4 jit_solution(11360306069729550579)
XLA Ops:
  0.0 1.7 %copy_bitcast_fusion = (bf16[128,512]{1,0:T(8,128)(2,1)}, bf16[128,512]{1,0:T(8,128)(2,1)}) fusion(bf16[16,8,4,128]{3,2,1,0:T(4,128)(2,1)} %bitcast.9, bf16[16,8,4,128]{3,2,1,0:T(4,128)(2,1)} %bitcast.10), kind=kLoop, calls=%fused_computation | loop fusion | bytes 524288 | tf_op jit(solution)/shard_map/reshape | solution.py:357
  1.7 59.1 %shard_map.82 = bf16[128,512]{1,0:T(8,128)(2,1)} custom-call(bf16[128,512]{1,0:T(8,128)(2,1)} %get-tuple-element.6.features, bf16[128,512]{1,0:T(8,128)(2,1)} %get-tuple-element.5.hidden, f32[1,128]{1,0:T(1,128)} %bitcast.11, f32[1,128]{1,0:T(1,128)} %bitcast.12, f32[1,128]{1,0:T(1,128)} %bitcast.13, bf16[3,3,128,2048]{3,2,1,0:T(8,128)(2,1)} %w_update.1, ...), custom_call_target="tpu_custom_call" | custom-call | tf_op jit(solution)/shard_map/pallas_call | solution.py:330
  60.8 1.6 %reshape.23 = bf16[128,4,128]{2,1,0:T(4,128)(2,1)} reshape(bf16[128,512]{1,0:T(8,128)(2,1)} %shard_map.82) | data formatting | bytes 262144 | tf_op jit(solution)/shard_map/reshape | solution.py:365
